TPU v7x, 32 devices: a whole 2x2x4 slice. The times are simulated.
32 devices in a mesh: orb: 16 (over z, x, core), aux: 2 (over y).
Axes of the slice: x: 2, y: 2, z: 4, core: 2. Of those that a mesh axis runs over, the one named last changes fastest.
Arguments:
- three_index: float32 [56, 1024, 2048], P(None, 'aux', 'orb'), may hold values from -0.5 to 0.5
- pair_density: float32 [3136, 3136], P('orb'), as said below
- active_orbitals: int32 [56], replicated, may hold values from 200 to 2047, as said below
- screen_mask: int32 [64, 128], P('aux', 'orb'), may hold values from 0 to 1
- one_density: float32 [56, 56], replicated
- inactive_fock: float32 [2048, 256], P('orb'), may hold values from -6 to 6
- active_fock: float32 [2048, 200], P('orb'), may hold values from -6 to 6
Outputs:
- rotation_gradient: float32 [2048, 256], P(('orb', 'aux'))
Inputs may be any that keep to these rules, and one draw needn't show every extreme that they name: `active_orbitals`: 56 distinct orbital indices. pair_density is symmetric: its entry at (tu, vw) equals that at (vw, tu).
All inputs are finite; a program needn't handle non-finite values.
Results may differ from a plain program's by a relative error of at most 0.0001.
Values sent between devices are 32-bit elements; how exact they have to be, the bound alone decides.
No kernel may reach another device: no remote copies, remote signals or barrier semaphores. Data moves between devices by JAX's collectives and lax.ppermute only.
A program may use at most 128 MiB of HBM per device.

v0:
```python
import jax
import jax.numpy as jnp
from jax import lax
from jax.sharding import PartitionSpec as P


def shards(
    three_index, pair_density, active_orbitals, screen_mask, one_density, inactive_fock, active_fock
):
    highest = lax.Precision.HIGHEST
    act_count = three_index.shape[0]
    slab_count = three_index.shape[1]
    row_count = three_index.shape[2]
    inactive_count = active_fock.shape[1]
    orb_position = lax.axis_index("orb")
    kept_mask = jnp.repeat(
        jnp.repeat(screen_mask.astype(jnp.float32), slab_count // screen_mask.shape[0], axis=0),
        row_count // screen_mask.shape[1],
        axis=1,
    )
    screened = three_index * kept_mask[None]
    global_rows = orb_position * row_count + jnp.arange(row_count, dtype=jnp.int32)
    active_pick = (global_rows[:, None] == active_orbitals[None, :]).astype(jnp.float32)
    partial_pairs = jnp.einsum("wPp,pv->Pvw", screened, active_pick, precision=highest).reshape(
        slab_count, act_count * act_count
    )
    pairs = lax.psum(partial_pairs, "orb")
    column_block = jnp.dot(pairs, pair_density.T, precision=highest)
    half = lax.all_gather(column_block, "orb", axis=1, tiled=True)
    q_partial = jnp.einsum(
        "uPp,Ptu->pt", screened, half.reshape(slab_count, act_count, act_count), precision=highest
    )
    occ_index = jnp.concatenate([jnp.arange(inactive_count, dtype=jnp.int32), active_orbitals])
    row_share = row_count // lax.axis_size("aux")
    aux_offset = lax.axis_index("aux") * row_share
    qmatrix = lax.psum(q_partial, "aux")
    inactive_cols = 2.0 * (inactive_fock[:, :inactive_count] + active_fock)
    active_cols = (
        jnp.dot(inactive_fock[:, inactive_count:], one_density, precision=highest) + qmatrix
    )
    fock = jnp.concatenate([inactive_cols, active_cols], axis=1)
    occ_pick = (global_rows[:, None] == occ_index[None, :]).astype(jnp.float32)
    occupied = lax.psum(jnp.dot(occ_pick.T, fock, precision=highest), "orb")
    fock_mine = lax.dynamic_slice_in_dim(fock, aux_offset, row_share, 0)
    pick_mine = lax.dynamic_slice_in_dim(occ_pick, aux_offset, row_share, 0)
    transposed = jnp.dot(pick_mine, occupied.T, precision=highest)
    return 2.0 * (fock_mine - transposed)


def solution(mesh):
    in_specs = (
        P(None, "aux", "orb"),
        P("orb", None),
        P(),
        P("aux", "orb"),
        P(),
        P("orb", None),
        P("orb", None),
    )
    out_specs = P(("orb", "aux"), None)
    return jax.shard_map(shards, mesh=mesh, in_specs=in_specs, out_specs=out_specs, check_vma=False)
```

profile of v0, /device:TPU:1, one launch (start us, length us, event | category | flops | bytes accessed | tf_op | source)
XLA Modules:
  0.0 370.7 jit_solution(4190907556177980599)
XLA Ops:
  6.5 0.8 convert_element_type.2
  7.4 0.1 broadcast_in_dim.4
  7.5 0.1 reshape.16
  7.6 0.1 copy.22
  7.8 13.5 %fusion.7 = f32[512,56,56]{0,1,2:T(8,128)S(1)} fusion(f32[56,512,128]{2,1,0:T(8,128)} %param.7, f32[512,128]{1,0:T(8,128)S(1)} %copy.22, s32[128]{0:T(128)S(1)} %iota_add_fusion, s32[56]{0:T(128)} %param.9), kind=kOutput, calls=%fused_computation.7 | convolution fusion | flops 2469927936 | bytes 21365472 | tf_op jit(solution)/shard_map/wPp,pv->Pvw/dot_general | solution.py:24
  21.2 6.4 %copy.23 = f32[512,56,56]{0,2,1:T(8,128)} copy(f32[512,56,56]{0,1,2:T(8,128)S(1)} %fusion.7) | data formatting | bytes 12845056 | tf_op jit(solution)/shard_map/wPp,pv->Pvw/transpose | solution.py:24
  27.6 0.0 all-reduce.3.cloned.1.call-update
  27.7 0.2 all-gather.3.cloned.1.call-start
  27.9 143.9 %all-reduce.3.cloned.1.call-done = f32[512,3136]{0,1:T(8,128)} async-done(((f32[512,3136]{0,1:T(8,128)}), f32[512,3136]{0,1:T(8,128)}) %all-reduce.3.cloned.1.call-update) | async-done | bytes 6422544 | tf_op jit(solution)/shard_map/psum | solution.py:27
  171.8 8.6 %convolution_bitcast_fusion = f32[1,196,512]{2,1,0:T(8,128)} fusion(f32[512,3136]{0,1:T(8,128)} %all-reduce.3.cloned.1.call-done, f32[196,3136]{1,0:T(8,128)S(1)} %copy-done), kind=kOutput, calls=%fused_computation.8 | convolution fusion | flops 3776446464 | bytes 9282560 | tf_op jit(solution)/shard_map/dot_general | solution.py:28
  180.4 0.0 all-gather.3.cloned.1.call-update
  180.4 0.0 all-reduce.5.cloned.1.call-start
  180.5 0.1 copy.21
  180.6 0.1 pad_add_fusion
  180.7 63.3 %all-gather.3.cloned.1.call-done = f32[16,196,512]{2,1,0:T(8,128)} async-done(((f32[1,196,512]{2,1,0:T(8,128)}), f32[16,196,512]{2,1,0:T(8,128)}) %all-gather.3.cloned.1.call-update) | async-done | bytes 6422544 | tf_op jit(solution)/shard_map/all_gather | solution.py:29
  244.0 6.1 %reshape.20 = f32[3136,512]{1,0:T(8,128)} reshape(f32[16,196,512]{2,1,0:T(8,128)} %all-gather.3.cloned.1.call-done) | data formatting | bytes 12845056
  250.2 15.4 %fusion.11 = f32[128,56]{0,1:T(8,128)S(1)} fusion(f32[512,56,56]{0,2,1:T(8,128)} %bitcast.23, f32[56,512,128]{2,1,0:T(8,128)} %param.7, f32[512,128]{1,0:T(8,128)S(1)} %copy.22), kind=kOutput, calls=%fused_computation.11 | convolution fusion | flops 2469920768 | bytes 21393408 | tf_op jit(solution)/shard_map/uPp,Ptu->pt/dot_general | solution.py:30
  265.5 6.3 %psum.22 = f32[128,56]{0,1:T(8,128)S(1)} all-reduce(f32[128,56]{0,1:T(8,128)S(1)} %fusion.11), channel_id=1, replica_groups=mesh['orb'=16,'aux'=2] {'aux'}, use_global_device_ids=true, to_apply=%region_1.0 | all-reduce | flops 7168 | bytes 57344 | tf_op jit(solution)/shard_map/psum | solution.py:36
  271.8 0.3 convolution_add_fusion
  272.2 0.1 copy.25
  272.3 1.1 fusion.16
  273.4 0.1 broadcast_compare_fusion
  273.5 88.9 %all-reduce.5.cloned.1.call-done = f32[256,256]{1,0:T(8,128)} async-done(((f32[256,256]{1,0:T(8,128)}), f32[256,256]{1,0:T(8,128)}) %all-reduce.5.cloned.1.call-update) | async-done | bytes 262160 | tf_op jit(solution)/shard_map/psum | solution.py:43
  362.3 1.9 fusion.10
  (16 shorter events, 0.1 us)
Async XLA Ops:
  6.5 165.2 %copy-start = (f32[196,3136]{1,0:T(8,128)S(1)}, f32[196,3136]{1,0:T(8,128)}, u32[]{:S(2)}) copy-start(f32[196,3136]{1,0:T(8,128)} %param.8) | copy-start | bytes 7375876
  6.5 165.2 %all-reduce.3.cloned.1.call-start = ((), (), s32[]{:S(2)}) async-start(), calls=%async_computation | async-start | bytes 12845056 | tf_op jit(solution)/shard_map/psum | solution.py:27
  27.6 152.8 %copy-start.2 = (f32[128,200]{0,1:T(8,128)S(1)}, f32[128,200]{0,1:T(8,128)}, u32[]{:S(2)}) copy-start(f32[128,200]{0,1:T(8,128)} %param.13) | copy-start | bytes 307204
  27.6 153.0 %copy-start.4 = (s32[56]{0:T(128)S(1)}, s32[56]{0:T(128)}, u32[]{:S(2)}) copy-start(s32[56]{0:T(128)} %param.9) | copy-start | bytes 676
  27.6 153.0 %copy-start.1 = (f32[128,256]{1,0:T(8,128)S(1)}, f32[128,256]{1,0:T(8,128)}, u32[]{:S(2)}) copy-start(f32[128,256]{1,0:T(8,128)} %param.12) | copy-start | bytes 393220
  27.7 216.4 %all-gather.3.cloned.1.call-start = ((), (), s32[]{:S(2)}) async-start(), calls=%async_computation.2 | async-start | bytes 6963200 | tf_op jit(solution)/shard_map/all_gather | solution.py:29
  180.4 181.9 %all-reduce.5.cloned.1.call-start = ((), (), s32[]{:S(2)}) async-start(), calls=%async_computation.1 | async-start | bytes 524288 | tf_op jit(solution)/shard_map/psum | solution.py:43
  250.2 21.7 %copy-start.3 = (f32[56,56]{1,0:T(8,128)S(1)}, f32[56,56]{1,0:T(8,128)}, u32[]{:S(2)}) copy-start(f32[56,56]{1,0:T(8,128)} %param.11) | copy-start | bytes 37636
Sparse Core Ops, SparseCore 0:
  27.7 143.9 all-reduce.2
  180.5 63.4 all-gather.2
  273.5 88.8 all-reduce.4
where the time goes:
time: 371 us
  waiting for transfers between devices  296 us (80%)
  matrix products  40.7 us (11%)
  between operations  13.2 us (4%)
  local copies, waits for them, and re-layouts  13 us (4%)
  blocking collectives  6.31 us (2%)
    psum x1, waiting for transfers between devices, shards(): pairs = lax.psum(partial_pairs, 'orb')  144 us
    psum x1, waiting for transfers between devices, shards(): occupied = lax.psum(jnp.dot(occ_pick.T, fock, precision=highest), 'orb')  88.9 us
    all_gather x1, waiting for transfers between devices, shards(): half = lax.all_gather(column_block, 'orb', axis=1, tiled=True)  63.3 us
    dot_general x1, matrix products, shards(): jnp.einsum('uPp,Ptu->pt', screened, half.reshape(slab_count, act_count, a...  15.4 us
    dot_general x1, matrix products, shards(): jnp.einsum('wPp,pv->Pvw', screened, active_pick, precision=highest)  13.5 us
    dot_general x1, matrix products, shards(): column_block = jnp.dot(pairs, pair_density.T, precision=highest)  8.61 us
  transfers between devices with their start and end apart: 3, of which 3 were waited for; matrix products, arithmetic and copies ran while one was open for 0% of the time, Pallas kernels for 0%

commit v1 on v0

--- a/solution.py
+++ b/solution.py
@@ -2,6 +2,30 @@
 import jax.numpy as jnp
 from jax import lax
 from jax.sharding import PartitionSpec as P
+
+
+def perform_the_cube(shard_in, device_axis, d0):
+    near, m_next, even = (
+        lax.axis_size(device_axis),
+        lax.axis_index(device_axis),
+        shard_in.shape[d0],
+    )
+    found = tuple((h * near if num == d0 else h for num, h in enumerate(shard_in.shape)))
+    w2 = lax.dynamic_update_slice_in_dim(
+        jnp.zeros(found, shard_in.dtype), shard_in, m_next * even, axis=d0
+    )
+    x_new = val = shard_in
+    for rr in [*range(1, near // 2 + 1)]:
+        x_new = lax.ppermute(
+            x_new, device_axis, perm=tuple(((num, (num + 1) % near) for num in range(near)))
+        )
+        w2 = lax.dynamic_update_slice_in_dim(w2, x_new, (m_next - rr) % near * even, axis=d0)
+        if 2 * rr < near:
+            val = lax.ppermute(
+                val, device_axis, perm=tuple(((num, (num - 1) % near) for num in range(near)))
+            )
+            w2 = lax.dynamic_update_slice_in_dim(w2, val, (m_next + rr) % near * even, axis=d0)
+    return w2
 
 
 def shards(
@@ -26,7 +50,7 @@
     )
     pairs = lax.psum(partial_pairs, "orb")
     column_block = jnp.dot(pairs, pair_density.T, precision=highest)
-    half = lax.all_gather(column_block, "orb", axis=1, tiled=True)
+    half = perform_the_cube(column_block, "orb", 1)
     q_partial = jnp.einsum(
         "uPp,Ptu->pt", screened, half.reshape(slab_count, act_count, act_count), precision=highest
     )

time: 371 us -> 420 us (1.13)
  local copies, waits for them, and re-layouts: 13 us -> 42.4 us
  starting transfers between devices: 0.27 us -> 19.3 us
    all_gather x1 -> x0, waiting for transfers between devices: 63.3 us -> none  [shards(): half = lax.all_gather(column_block, 'orb', axis=1, tiled=True)]
    ppermute x0 -> x15, waiting for transfers between devices: none -> 61.6 us  [the longest x8 61.1 us: perform_the_cube(): lax.ppermute(x_new, device_axis, perm=tuple(((num, (num + 1) % near) for...]
    dynamic_update_slice x0 -> x16, local copies, waits for them, and re-layouts: none -> 31 us  [the longest x8 15.5 us: perform_the_cube(): lax.dynamic_update_slice_in_dim(w2, x_new, (m_next - rr) % near * even, a...]
    ppermute x0 -> x15, starting transfers between devices: none -> 19.3 us  [the longest x8 19.1 us: perform_the_cube(): lax.ppermute(x_new, device_axis, perm=tuple(((num, (num + 1) % near) for...]
    unnamed x12 -> x33, local copies, waits for them, and re-layouts: 6.23 us -> 1.06 us
  transfers between devices with their start and end apart: 3 -> 17, of which waited for: 3 -> 11; matrix products, arithmetic and copies ran while one was open for 0% -> 8% of each run, Pallas kernels for 0% -> 0%
where the time goes in v1:
time: 420 us; the launch traced here: 419 us
  waiting for transfers between devices  296 us (70%)
  local copies, waits for them, and re-layouts  42.4 us (10%)
  matrix products  39.3 us (9%)
  starting transfers between devices  19.3 us (5%)
  between operations  14 us (3%)
  blocking collectives  6.31 us (2%)
    psum x1, waiting for transfers between devices, shards(): pairs = lax.psum(partial_pairs, 'orb')  144 us
    psum x1, waiting for transfers between devices, shards(): occupied = lax.psum(jnp.dot(occ_pick.T, fock, precision=highest), 'orb')  90.4 us
    ppermute x8, waiting for transfers between devices, perform_the_cube(): lax.ppermute(x_new, device_axis, perm=tuple(((num, (num + 1) % near) for...  61.1 us
    ppermute x8, starting transfers between devices, perform_the_cube(): lax.ppermute(x_new, device_axis, perm=tuple(((num, (num + 1) % near) for...  19.1 us
    dynamic_update_slice x8, local copies, waits for them, and re-layouts, perform_the_cube(): lax.dynamic_update_slice_in_dim(w2, x_new, (m_next - rr) % near * even, a...  15.5 us
    dot_general x1, matrix products, shards(): jnp.einsum('uPp,Ptu->pt', screened, half.reshape(slab_count, act_count, a...  15.4 us
    dynamic_update_slice x7, local copies, waits for them, and re-layouts, perform_the_cube(): lax.dynamic_update_slice_in_dim(w2, val, (m_next + rr) % near * even, axi...  13.6 us
    dot_general x1, matrix products, shards(): jnp.einsum('wPp,pv->Pvw', screened, active_pick, precision=highest)  13.5 us
  transfers between devices with their start and end apart: 17, of which 11 were waited for; matrix products, arithmetic and copies ran while one was open for 8% of the time, Pallas kernels for 0%

profile of v1, /device:TPU:1, one launch (start us, length us, event | category | flops | bytes accessed | tf_op | source)
XLA Modules:
  0.0 419.3 jit_solution(9614864921741960523)
XLA Ops:
  7.8 13.5 %fusion.7 = f32[512,56,56]{0,1,2:T(8,128)S(1)} fusion(f32[56,512,128]{2,1,0:T(8,128)} %param.7, f32[512,128]{1,0:T(8,128)S(1)} %copy.17, s32[128]{0:T(128)S(1)} %iota_add_fusion, s32[56]{0:T(128)} %param.9), kind=kOutput, calls=%fused_computation.7 | convolution fusion | flops 2469927936 | bytes 21365472 | tf_op jit(solution)/shard_map/wPp,pv->Pvw/dot_general | solution.py:48
  21.2 6.4 %copy.18 = f32[512,56,56]{0,2,1:T(8,128)} copy(f32[512,56,56]{0,1,2:T(8,128)S(1)} %fusion.7) | data formatting | bytes 12845056 | tf_op jit(solution)/shard_map/wPp,pv->Pvw/transpose | solution.py:48
  27.7 144.1 %all-reduce.3.cloned.1.call-done = f32[512,3136]{0,1:T(8,128)} async-done(((f32[512,3136]{0,1:T(8,128)}), f32[512,3136]{0,1:T(8,128)}) %all-reduce.3.cloned.1.call-update) | async-done | bytes 6422544 | tf_op jit(solution)/shard_map/psum | solution.py:51
  171.8 7.3 %fusion.28 = f32[512,196]{0,1:T(8,128)S(1)} fusion(f32[512,3136]{0,1:T(8,128)} %all-reduce.3.cloned.1.call-done, f32[196,3136]{1,0:T(8,128)S(1)} %copy-done), kind=kOutput, calls=%fused_computation.30 | convolution fusion | flops 3776446464 | bytes 9282560 | tf_op jit(solution)/shard_map/dot_general | solution.py:52
  180.7 9.3 %collective-permute-done = f32[512,196]{0,1:T(8,128)S(1)} collective-permute-done((f32[512,196]{0,1:T(8,128)S(1)}, f32[512,196]{0,1:T(8,128)S(1)}, u32[]{:S(2)}, u32[]{:S(2)}) %collective-permute-start) | collective-permute-done | bytes 401440 | tf_op jit(solution)/shard_map/ppermute | solution.py:19
  190.0 2.5 collective-permute-start.2
  192.5 8.3 %collective-permute-done.2 = f32[512,196]{0,1:T(8,128)S(1)} collective-permute-done((f32[512,196]{0,1:T(8,128)S(1)}, f32[512,196]{0,1:T(8,128)S(1)}, u32[]{:S(2)}, u32[]{:S(2)}) %collective-permute-start.2) | collective-permute-done | bytes 401440 | tf_op jit(solution)/shard_map/ppermute | solution.py:19
  200.9 2.5 collective-permute-start.4
  203.6 8.4 %collective-permute-done.4 = f32[512,196]{0,1:T(8,128)S(1)} collective-permute-done((f32[512,196]{0,1:T(8,128)S(1)}, f32[512,196]{0,1:T(8,128)S(1)}, u32[]{:S(2)}, u32[]{:S(2)}) %collective-permute-start.4) | collective-permute-done | bytes 401440 | tf_op jit(solution)/shard_map/ppermute | solution.py:19
  212.0 2.5 collective-permute-start.6
  214.5 12.0 %collective-permute-done.6 = f32[512,196]{0,1:T(8,128)S(1)} collective-permute-done((f32[512,196]{0,1:T(8,128)S(1)}, f32[512,196]{0,1:T(8,128)S(1)}, u32[]{:S(2)}, u32[]{:S(2)}) %collective-permute-start.6) | collective-permute-done | bytes 401440 | tf_op jit(solution)/shard_map/ppermute | solution.py:19
  226.5 2.5 collective-permute-start.8
  229.1 9.2 %collective-permute-done.8 = f32[512,196]{0,1:T(8,128)S(1)} collective-permute-done((f32[512,196]{0,1:T(8,128)S(1)}, f32[512,196]{0,1:T(8,128)S(1)}, u32[]{:S(2)}, u32[]{:S(2)}) %collective-permute-start.8) | collective-permute-done | bytes 401440 | tf_op jit(solution)/shard_map/ppermute | solution.py:19
  238.3 2.5 collective-permute-start.10
  240.8 9.2 %collective-permute-done.10 = f32[512,196]{0,1:T(8,128)S(1)} collective-permute-done((f32[512,196]{0,1:T(8,128)S(1)}, f32[512,196]{0,1:T(8,128)S(1)}, u32[]{:S(2)}, u32[]{:S(2)}) %collective-permute-start.10) | collective-permute-done | bytes 401440 | tf_op jit(solution)/shard_map/ppermute | solution.py:19
  250.1 2.5 collective-permute-start.12
  252.7 4.7 %collective-permute-done.12 = f32[512,196]{0,1:T(8,128)} collective-permute-done((f32[512,196]{0,1:T(8,128)S(1)}, f32[512,196]{0,1:T(8,128)}, u32[]{:S(2)}, u32[]{:S(2)}) %collective-permute-start.12) | collective-permute-done | bytes 401440 | tf_op jit(solution)/shard_map/ppermute | solution.py:19
  257.4 2.6 collective-permute-start.14
  262.8 3.5 broadcast_in_dim.15
  268.1 2.0 dynamic_update_slice.49
  279.8 2.0 dynamic_update_slice.55
  297.3 15.4 %fusion.11 = f32[128,56]{0,1:T(8,128)S(1)} fusion(f32[512,56,56]{0,2,1:T(8,128)} %bitcast.17, f32[56,512,128]{2,1,0:T(8,128)} %param.7, f32[512,128]{1,0:T(8,128)S(1)} %copy.17), kind=kOutput, calls=%fused_computation.10 | convolution fusion | flops 2469920768 | bytes 21393408 | tf_op jit(solution)/shard_map/uPp,Ptu->pt/dot_general | solution.py:54
  312.6 6.3 %psum.22 = f32[128,56]{0,1:T(8,128)S(1)} all-reduce(f32[128,56]{0,1:T(8,128)S(1)} %fusion.11), channel_id=1, replica_groups=mesh['orb'=16,'aux'=2] {'aux'}, use_global_device_ids=true, to_apply=%region_1.2 | all-reduce | flops 7168 | bytes 57344 | tf_op jit(solution)/shard_map/psum | solution.py:60
  320.3 90.4 %all-reduce.5.cloned.1.call-done = f32[256,256]{1,0:T(8,128)} async-done(((f32[256,256]{1,0:T(8,128)}), f32[256,256]{1,0:T(8,128)}) %all-reduce.5.cloned.1.call-update) | async-done | bytes 262160 | tf_op jit(solution)/shard_map/psum | solution.py:67
  (82 shorter events, 36.1 us)
Async XLA Ops:
  6.5 165.3 %copy-start = (f32[196,3136]{1,0:T(8,128)S(1)}, f32[196,3136]{1,0:T(8,128)}, u32[]{:S(2)}) copy-start(f32[196,3136]{1,0:T(8,128)} %param.8) | copy-start | bytes 7375876
  6.5 165.3 %all-reduce.3.cloned.1.call-start = ((), (), s32[]{:S(2)}) async-start(), calls=%async_computation | async-start | bytes 12845056 | tf_op jit(solution)/shard_map/psum | solution.py:51
  27.6 232.4 %copy-start.13 = (f32[128,256]{1,0:T(8,128)S(1)}, f32[128,256]{1,0:T(8,128)}, u32[]{:S(2)}) copy-start(f32[128,256]{1,0:T(8,128)} %param.12) | copy-start | bytes 393220
  27.7 232.4 %copy-start.14 = (f32[56,56]{1,0:T(8,128)S(1)}, f32[56,56]{1,0:T(8,128)}, u32[]{:S(2)}) copy-start(f32[56,56]{1,0:T(8,128)} %param.11) | copy-start | bytes 37636
  27.7 234.1 %copy-start.15 = (s32[56]{0:T(128)S(1)}, s32[56]{0:T(128)}, u32[]{:S(2)}) copy-start(s32[56]{0:T(128)} %param.9) | copy-start | bytes 676
  27.7 382.9 %all-reduce.5.cloned.1.call-start = ((), (), s32[]{:S(2)}) async-start(), calls=%async_computation.1 | async-start | bytes 524288 | tf_op jit(solution)/shard_map/psum | solution.py:67
  179.1 10.9 %collective-permute-start = (f32[512,196]{0,1:T(8,128)S(1)}, f32[512,196]{0,1:T(8,128)S(1)}, u32[]{:S(2)}, u32[]{:S(2)}) collective-permute-start(f32[512,196]{0,1:T(8,128)S(1)} %fusion.28), channel_id=1, source_target_pairs={{0,2},{2,4},{4,6},{6,8},{8,10},{10,12},{12,14},{14,16},{16,18},{18... | collective-permute-start | bytes 1204232 | tf_op jit(solution)/shard_map/ppermute | solution.py:19
  180.7 11.8 %collective-permute-start.1 = (f32[512,196]{0,1:T(8,128)S(1)}, f32[512,196]{0,1:T(8,128)S(1)}, u32[]{:S(2)}, u32[]{:S(2)}) collective-permute-start(f32[512,196]{0,1:T(8,128)S(1)} %fusion.28), channel_id=1, source_target_pairs={{0,30},{2,0},{4,2},{6,4},{8,6},{10,8},{12,10},{14,12},{16,14},{18,... | collective-permute-start | bytes 1204232 | tf_op jit(solution)/shard_map/ppermute | solution.py:24
  190.0 10.9 %collective-permute-start.2 = (f32[512,196]{0,1:T(8,128)S(1)}, f32[512,196]{0,1:T(8,128)S(1)}, u32[]{:S(2)}, u32[]{:S(2)}) collective-permute-start(f32[512,196]{0,1:T(8,128)S(1)} %collective-permute-done), channel_id=1, source_target_pairs={{0,2},{2,4},{4,6},{6,8},{8,10},{10,12},{12,14},{14,16},{16,18},{18... | collective-permute-start | bytes 1204232 | tf_op jit(solution)/shard_map/ppermute | solution.py:19
  192.5 11.1 %collective-permute-start.3 = (f32[512,196]{0,1:T(8,128)S(1)}, f32[512,196]{0,1:T(8,128)S(1)}, u32[]{:S(2)}, u32[]{:S(2)}) collective-permute-start(f32[512,196]{0,1:T(8,128)S(1)} %collective-permute-done.1), channel_id=1, source_target_pairs={{0,30},{2,0},{4,2},{6,4},{8,6},{10,8},{12,10},{14,12},{16,14},{18,... | collective-permute-start | bytes 1204232 | tf_op jit(solution)/shard_map/ppermute | solution.py:24
  200.9 11.1 %collective-permute-start.4 = (f32[512,196]{0,1:T(8,128)S(1)}, f32[512,196]{0,1:T(8,128)S(1)}, u32[]{:S(2)}, u32[]{:S(2)}) collective-permute-start(f32[512,196]{0,1:T(8,128)S(1)} %collective-permute-done.2), channel_id=1, source_target_pairs={{0,2},{2,4},{4,6},{6,8},{8,10},{10,12},{12,14},{14,16},{16,18},{18... | collective-permute-start | bytes 1204232 | tf_op jit(solution)/shard_map/ppermute | solution.py:19
  203.6 10.9 %collective-permute-start.5 = (f32[512,196]{0,1:T(8,128)S(1)}, f32[512,196]{0,1:T(8,128)S(1)}, u32[]{:S(2)}, u32[]{:S(2)}) collective-permute-start(f32[512,196]{0,1:T(8,128)S(1)} %collective-permute-done.3), channel_id=1, source_target_pairs={{0,30},{2,0},{4,2},{6,4},{8,6},{10,8},{12,10},{14,12},{16,14},{18,... | collective-permute-start | bytes 1204232 | tf_op jit(solution)/shard_map/ppermute | solution.py:24
  212.0 14.5 %collective-permute-start.6 = (f32[512,196]{0,1:T(8,128)S(1)}, f32[512,196]{0,1:T(8,128)S(1)}, u32[]{:S(2)}, u32[]{:S(2)}) collective-permute-start(f32[512,196]{0,1:T(8,128)S(1)} %collective-permute-done.4), channel_id=1, source_target_pairs={{0,2},{2,4},{4,6},{6,8},{8,10},{10,12},{12,14},{14,16},{16,18},{18... | collective-permute-start | bytes 1204232 | tf_op jit(solution)/shard_map/ppermute | solution.py:19
  214.5 12.0 %copy-start.6 = (f32[512,196]{0,1:T(8,128)}, f32[512,196]{0,1:T(8,128)S(1)}, u32[]{:S(2)}) copy-start(f32[512,196]{0,1:T(8,128)S(1)} %collective-permute-done.5) | copy-start | bytes 1204228
  214.5 14.5 %collective-permute-start.7 = (f32[512,196]{0,1:T(8,128)S(1)}, f32[512,196]{0,1:T(8,128)S(1)}, u32[]{:S(2)}, u32[]{:S(2)}) collective-permute-start(f32[512,196]{0,1:T(8,128)S(1)} %collective-permute-done.5), channel_id=1, source_target_pairs={{0,30},{2,0},{4,2},{6,4},{8,6},{10,8},{12,10},{14,12},{16,14},{18,... | collective-permute-start | bytes 1204232 | tf_op jit(solution)/shard_map/ppermute | solution.py:24
  226.5 11.8 %collective-permute-start.8 = (f32[512,196]{0,1:T(8,128)S(1)}, f32[512,196]{0,1:T(8,128)S(1)}, u32[]{:S(2)}, u32[]{:S(2)}) collective-permute-start(f32[512,196]{0,1:T(8,128)S(1)} %collective-permute-done.6), channel_id=1, source_target_pairs={{0,2},{2,4},{4,6},{6,8},{8,10},{10,12},{12,14},{14,16},{16,18},{18... | collective-permute-start | bytes 1204232 | tf_op jit(solution)/shard_map/ppermute | solution.py:19
  229.0 9.3 %copy-start.8 = (f32[512,196]{0,1:T(8,128)}, f32[512,196]{0,1:T(8,128)S(1)}, u32[]{:S(2)}) copy-start(f32[512,196]{0,1:T(8,128)S(1)} %collective-permute-done.7) | copy-start | bytes 1204228
  229.0 11.8 %collective-permute-start.9 = (f32[512,196]{0,1:T(8,128)S(1)}, f32[512,196]{0,1:T(8,128)S(1)}, u32[]{:S(2)}, u32[]{:S(2)}) collective-permute-start(f32[512,196]{0,1:T(8,128)S(1)} %collective-permute-done.7), channel_id=1, source_target_pairs={{0,30},{2,0},{4,2},{6,4},{8,6},{10,8},{12,10},{14,12},{16,14},{18,... | collective-permute-start | bytes 1204232 | tf_op jit(solution)/shard_map/ppermute | solution.py:24
  238.3 11.8 %collective-permute-start.10 = (f32[512,196]{0,1:T(8,128)S(1)}, f32[512,196]{0,1:T(8,128)S(1)}, u32[]{:S(2)}, u32[]{:S(2)}) collective-permute-start(f32[512,196]{0,1:T(8,128)S(1)} %collective-permute-done.8), channel_id=1, source_target_pairs={{0,2},{2,4},{4,6},{6,8},{8,10},{10,12},{12,14},{14,16},{16,18},{18... | collective-permute-start | bytes 1204232 | tf_op jit(solution)/shard_map/ppermute | solution.py:19
  240.8 11.9 %collective-permute-start.11 = (f32[512,196]{0,1:T(8,128)S(1)}, f32[512,196]{0,1:T(8,128)}, u32[]{:S(2)}, u32[]{:S(2)}) collective-permute-start(f32[512,196]{0,1:T(8,128)S(1)} %collective-permute-done.9), channel_id=1, source_target_pairs={{0,30},{2,0},{4,2},{6,4},{8,6},{10,8},{12,10},{14,12},{16,14},{18,... | collective-permute-start | bytes 1204232 | tf_op jit(solution)/shard_map/ppermute | solution.py:24
  250.1 7.4 %collective-permute-start.12 = (f32[512,196]{0,1:T(8,128)S(1)}, f32[512,196]{0,1:T(8,128)}, u32[]{:S(2)}, u32[]{:S(2)}) collective-permute-start(f32[512,196]{0,1:T(8,128)S(1)} %collective-permute-done.10), channel_id=1, source_target_pairs={{0,2},{2,4},{4,6},{6,8},{8,10},{10,12},{12,14},{14,16},{16,18},{18... | collective-permute-start | bytes 1204232 | tf_op jit(solution)/shard_map/ppermute | solution.py:19
  252.7 40.6 %collective-permute-start.13 = (f32[512,196]{0,1:T(8,128)}, f32[512,196]{0,1:T(8,128)}, u32[]{:S(2)}, u32[]{:S(2)}) collective-permute-start(f32[512,196]{0,1:T(8,128)} %collective-permute-done.11), channel_id=1, source_target_pairs={{0,30},{2,0},{4,2},{6,4},{8,6},{10,8},{12,10},{14,12},{16,14},{18,... | collective-permute-start | bytes 1204232 | tf_op jit(solution)/shard_map/ppermute | solution.py:24
  257.4 37.9 %collective-permute-start.14 = (f32[512,196]{0,1:T(8,128)}, f32[512,196]{0,1:T(8,128)}, u32[]{:S(2)}, u32[]{:S(2)}) collective-permute-start(f32[512,196]{0,1:T(8,128)} %collective-permute-done.12), channel_id=1, source_target_pairs={{0,2},{2,4},{4,6},{6,8},{8,10},{10,12},{12,14},{14,16},{16,18},{18... | collective-permute-start | bytes 1204232 | tf_op jit(solution)/shard_map/ppermute | solution.py:19
  268.1 15.6 %copy-start.10 = (f32[512,196]{0,1:T(8,128)S(1)}, f32[512,196]{0,1:T(8,128)}, u32[]{:S(2)}) copy-start(f32[512,196]{0,1:T(8,128)} %copy-done.9) | copy-start | bytes 1204228
  (9 other events, 41.4 us)
Sparse Core Ops, SparseCore 0:
  27.8 143.9 all-reduce.2
  320.3 90.2 all-reduce.4
